TPU v7x, 256 devices: a whole 4x4x8 slice. The times are simulated.
256 devices in a mesh: tm: 32 (over x, y, core), row: 8 (over z).
Axes of the slice: x: 4, y: 4, z: 8, core: 2. Of those that a mesh axis runs over, the one named last changes fastest.
Arguments:
- frames_in: bfloat16 [64, 32, 64, 256], P('tm', 'row'), may hold values from -6 to 6
- cotangent: bfloat16 [64, 32, 64, 256], P('tm', 'row'), may hold values from -6 to 6
- kernel: bfloat16 [9, 256, 256], replicated, may hold values from -0.125 to 0.125
- readout: bfloat16 [256, 256], replicated, may hold values from -0.375 to 0.375
- feedthrough: float32 [256], replicated, may hold values from 0.5 to 1.5
- decay_rate: float32 [64, 256], P('tm'), may hold values from 0.05 to 1, as said below
- start_state: float32 [32, 64, 256], P('row'), may hold values from -6 to 6
Outputs:
- grad_frames: bfloat16 [64, 32, 64, 256], P('tm', 'row')
- grad_kernel: float32 [9, 256, 256], P(None, 'row')
- grad_readout: float32 [256, 256], P(None, 'row')
Inputs may be any that keep to these rules, and one draw needn't show every extreme that they name: `decay_rate`: every entry lies strictly between 0 and 1.
All inputs are finite; a program needn't handle non-finite values.
Results may differ from a plain program's by a relative error of at most 0.015.
Values may be sent and summed in bfloat16 or wider, within the bound.
No kernel may reach another device: no remote copies, remote signals or barrier semaphores. Data moves between devices by JAX's collectives and lax.ppermute only.
A program may use at most 64 MiB of HBM per device.

v0:
```python
import math
import jax
import jax.numpy as jnp
from jax import lax
from jax.sharding import PartitionSpec as P

SQRT_TWO_PI = 0.7978845608
CUBIC = 0.044715


def extended(cells, sides, width):
    for axis, dim in sides:
        count = lax.axis_size(axis)
        ends = count - 1
        head = lax.slice_in_dim(cells, 0, width, axis=dim)
        tail = lax.slice_in_dim(cells, cells.shape[dim] - width, cells.shape[dim], axis=dim)
        cells = jnp.concatenate(
            [
                lax.ppermute(tail, axis, [(i, (i + 1) % count) for i in range(ends)]),
                cells,
                lax.ppermute(head, axis, [((i + 1) % count, i) for i in range(ends)]),
            ],
            axis=dim,
        )
    return cells


def carried_in(value, axis, join, neutral, backward):
    count, mine = (lax.axis_size(axis), lax.axis_index(axis))
    pieces = jax.tree.map(lambda part: lax.all_gather(part, axis), value)
    if backward:
        pieces = jax.tree.map(lambda part: part[::-1], pieces)
        mine = count - 1 - mine
    subtotal = jax.tree.map(
        lambda part, zero: jnp.full_like(part, 0) + jnp.asarray(zero, part.dtype), value, neutral
    )

    def turn(position, subtotal):
        longer = join(subtotal, jax.tree.map(lambda part: part[position], pieces))
        return jax.tree.map(lambda new, old: jnp.where(position < mine, new, old), longer, subtotal)

    return lax.fori_loop(0, count - 1, turn, subtotal)


def gelu_slope(mixture):
    inside = SQRT_TWO_PI * (mixture + CUBIC * mixture * mixture * mixture)
    tangent = jnp.tanh(inside)
    return 0.5 * (1.0 + tangent) + 0.5 * mixture * (1.0 - tangent * tangent) * SQRT_TWO_PI * (
        1.0 + 3.0 * CUBIC * mixture * mixture
    )


def block_taps(padded, band_rows, grid_width, flipped):
    pieces = []
    for vertical in range(3):
        for lateral in range(3):
            from_top = 2 - vertical if flipped else vertical
            from_left = 2 - lateral if flipped else lateral
            pieces.append(
                padded[:, from_top : from_top + band_rows, from_left : from_left + grid_width, :]
            )
    return jnp.stack(pieces, axis=3)


def compose(earlier, later):
    return (later[0] * earlier[0], later[0] * earlier[1] + later[1])


def local(frames_in, cotangent, kernel, readout, feedthrough, decay_rate, start_state):
    frames_here, band_rows, grid_width, channels = frames_in.shape
    state_width = kernel.shape[2]
    cell_count = frames_here * band_rows * grid_width
    rimmed = extended(frames_in, (("row", 1),), 1)
    padded = jnp.pad(rimmed, ((0, 0), (0, 0), (1, 1), (0, 0)))
    input_taps = block_taps(padded, band_rows, grid_width, False).reshape(cell_count, 9 * channels)
    driven = jnp.dot(
        input_taps, kernel.reshape(9 * channels, state_width), preferred_element_type=jnp.float32
    )
    driven = driven.reshape(frames_here, band_rows, grid_width, state_width)
    gain_all = jnp.sqrt(1.0 - decay_rate * decay_rate)
    leader = (lax.axis_index("tm") == 0).astype(jnp.float32)

    def advance(carried, inputs):
        driven_now, rate_now, gain_now = inputs
        carried = rate_now * carried + gain_now * driven_now
        return (carried, carried)

    _, local_states = lax.scan(advance, start_state * leader, (driven, decay_rate, gain_all))
    through = jnp.cumprod(decay_rate, axis=0)
    identity = (
        jnp.ones((state_width,), jnp.float32),
        jnp.zeros((band_rows, grid_width, state_width), jnp.float32),
    )
    _, entering = carried_in((through[-1], local_states[-1]), "tm", compose, identity, False)
    states = local_states + through[:, None, None, :] * entering[None]
    state_bf = states.astype(jnp.bfloat16).reshape(cell_count, state_width)
    mixture = jnp.dot(state_bf, readout, preferred_element_type=jnp.float32)
    slope_bf = (
        cotangent.reshape(cell_count, channels).astype(jnp.float32) * gelu_slope(mixture)
    ).astype(jnp.bfloat16)
    pulled = lax.dot_general(
        slope_bf, readout, (((1,), (1,)), ((), ())), preferred_element_type=jnp.float32
    )
    pulled = pulled.reshape(frames_here, band_rows, grid_width, state_width)
    later_rate = jnp.concatenate([decay_rate[1:], jnp.ones((1, state_width), jnp.float32)], axis=0)

    def retreat(carried, inputs):
        pulled_now, rate_next = inputs
        carried = pulled_now + rate_next * carried
        return (carried, carried)

    _, local_adjoint = lax.scan(
        retreat,
        jnp.zeros((band_rows, grid_width, state_width), jnp.float32),
        (pulled, later_rate),
        reverse=True,
    )
    remaining = jnp.flip(jnp.cumprod(jnp.flip(later_rate, 0), axis=0), 0)
    _, arriving = carried_in(
        (through[-1], decay_rate[0][None, None, :] * local_adjoint[0]),
        "tm",
        compose,
        identity,
        True,
    )
    adjoint = local_adjoint + remaining[:, None, None, :] * arriving[None]
    grad_drive = (gain_all[:, None, None, :] * adjoint).astype(jnp.bfloat16)
    rim_adjoint = extended(grad_drive, (("row", 1),), 1)
    padded_drive = jnp.pad(rim_adjoint, ((0, 0), (0, 0), (1, 1), (0, 0)))
    output_taps = block_taps(padded_drive, band_rows, grid_width, True).reshape(
        cell_count, 9, state_width
    )
    spread = lax.dot_general(
        output_taps, kernel, (((1, 2), (0, 2)), ((), ())), preferred_element_type=jnp.float32
    )
    spread = spread.reshape(frames_here, band_rows, grid_width, channels)
    grad_frames = (spread + feedthrough * cotangent.astype(jnp.float32)).astype(jnp.bfloat16)
    kernel_term = lax.dot_general(
        input_taps,
        grad_drive.reshape(cell_count, state_width),
        (((0,), (0,)), ((), ())),
        preferred_element_type=jnp.float32,
    ).reshape(9, channels, state_width)
    readout_term = lax.dot_general(
        state_bf, slope_bf, (((0,), (0,)), ((), ())), preferred_element_type=jnp.float32
    )
    band_count = lax.axis_size("row")
    scaling = 1.0 / math.sqrt(cell_count * lax.axis_size("tm") * band_count)
    share_width = channels // band_count
    kernel_all, readout_all = lax.psum((kernel_term, readout_term), ("tm", "row"))
    offset_start = lax.axis_index("row") * share_width
    kernel_part = lax.dynamic_slice_in_dim(kernel_all, offset_start, share_width, 1)
    readout_part = lax.dynamic_slice_in_dim(readout_all, offset_start, share_width, 1)
    return (grad_frames, kernel_part * scaling, readout_part * scaling)


def solution(mesh):
    placed = (
        P("tm", "row", None, None),
        P("tm", "row", None, None),
        P(),
        P(),
        P(),
        P("tm", None),
        P("row", None, None),
    )
    return jax.shard_map(
        local,
        mesh=mesh,
        in_specs=placed,
        out_specs=(P("tm", "row", None, None), P(None, "row", None), P(None, "row")),
        check_vma=False,
    )
```

profile of v0, /device:TPU:2, one launch (start us, length us, event | category | flops | bytes accessed | tf_op | source)
XLA Modules:
  0.0 510.4 jit_solution(2149309793703916554)
XLA Ops:
  8.2 3.8 collective-permute-start
  12.1 1.3 collective-permute-start.1
  15.1 3.2 collective-permute-done.1
  23.3 24.2 %all-gather = f32[32,1,256]{2,1,0:T(1,128)S(1)} all-gather(f32[1,1,256]{2,1,0:T(1,128)S(1)} %slice_bitcast_fusion.12), channel_id=1, replica_groups=mesh['tm'=32,'row'=8] {'tm'}, dimensions={0}, use_global_device_ids=true | all-gather | bytes 33792 | tf_op jit(solution)/shard_map/all_gather | solution.py:30
  47.6 36.4 %all-gather.4.cloned.1.call-done = f32[32,4,64,256]{3,2,1,0:T(8,128)} async-done(((f32[1,4,64,256]{3,2,1,0:T(8,128)}), f32[32,4,64,256]{3,2,1,0:T(8,128)}) %all-gather.4.cloned.1.call-update) | async-done | bytes 8388624 | tf_op jit(solution)/shard_map/all_gather | solution.py:30
  84.0 36.9 %while.58 = (s32[]{:T(128)}, f32[4,64,256]{2,1,0:T(8,128)S(1)}, s32[]{:T(128)}, f32[32,256]{1,0:T(8,128)S(1)}, f32[32,4,64,256]{3,2,1,0:T(8,128)}, /*index=5*/s32[]{:T(128)}, s32[]{:T(128)}) while((s32[]{:T(128)}, f32[4,64,256]{2,1,0:T(8,128)S(1)}, s32[]{:T(128)}, f32[32,256]{1,0:T(8,128)S(1)}, f32[32,4,64,256]{3,2,1,0:T(8,128)}, ...), condition=%wide.region_4.5_spmd.clone, body=%wide.region_3.4_spmd.clone.sunk | while | flops 262148 | bytes 789609 | solution.py:42
  84.0 1.2 fusion.59
  85.2 1.1 fusion.59
  86.4 1.1 fusion.59
  87.6 1.1 fusion.59
  88.8 1.1 fusion.59
  90.0 1.1 fusion.59
  91.2 1.1 fusion.59
  92.4 1.1 fusion.59
  93.5 1.1 fusion.59
  94.7 1.1 fusion.59
  95.9 1.1 fusion.59
  97.1 1.1 fusion.59
  98.3 1.1 fusion.59
  99.5 1.1 fusion.59
  100.7 1.1 fusion.59
  101.9 1.1 fusion.59
  103.1 1.1 fusion.59
  104.3 1.1 fusion.59
  105.4 1.1 fusion.59
  106.6 1.1 fusion.59
  107.8 1.1 fusion.59
  109.0 1.1 fusion.59
  110.2 1.1 fusion.59
  111.4 1.1 fusion.59
  112.6 1.1 fusion.59
  113.8 1.1 fusion.59
  115.0 1.1 fusion.59
  116.1 1.1 fusion.59
  117.3 1.1 fusion.59
  118.5 1.1 fusion.59
  119.7 1.1 fusion.59
  123.2 3.3 copy.51
  126.5 2.8 copy.57
  129.3 4.3 copy.52
  134.5 45.9 %all-gather.6.cloned.1.call-done = f32[32,4,64,256]{3,2,1,0:T(8,128)} async-done(((f32[1,4,64,256]{3,2,1,0:T(8,128)}), f32[32,4,64,256]{3,2,1,0:T(8,128)}) %all-gather.6.cloned.1.call-update) | async-done | bytes 8388624 | tf_op jit(solution)/shard_map/all_gather | solution.py:30
  180.4 7.7 %rev.16 = f32[32,4,64,256]{3,2,1,0:T(8,128)} reverse(f32[32,4,64,256]{3,2,1,0:T(8,128)} %all-gather.6.cloned.1.call-done), dimensions={0} | reverse | bytes 16777216 | tf_op jit(solution)/shard_map/rev | solution.py:32
  188.1 36.8 %while.60 = (s32[]{:T(128)}, f32[4,64,256]{2,1,0:T(8,128)S(1)}, s32[]{:T(128)}, f32[32,256]{1,0:T(8,128)S(1)}, f32[32,4,64,256]{3,2,1,0:T(8,128)}, /*index=5*/s32[]{:T(128)}, s32[]{:T(128)}) while((s32[]{:T(128)}, f32[4,64,256]{2,1,0:T(8,128)S(1)}, s32[]{:T(128)}, f32[32,256]{1,0:T(8,128)S(1)}, f32[32,4,64,256]{3,2,1,0:T(8,128)}, ...), condition=%wide.region_9.10_spmd.clone, body=%wide.region_8.9_spmd.clone.sunk | while | flops 262148 | bytes 789609 | solution.py:42
  189.3 1.1 fusion.60
  190.5 1.1 fusion.60
  191.7 1.1 fusion.60
  192.9 1.1 fusion.60
  194.1 1.1 fusion.60
  195.3 1.1 fusion.60
  196.5 1.1 fusion.60
  197.7 1.1 fusion.60
  198.8 1.1 fusion.60
  200.0 1.1 fusion.60
  201.2 1.1 fusion.60
  202.4 1.1 fusion.60
  203.6 1.1 fusion.60
  204.8 1.1 fusion.60
  225.1 3.5 collective-permute-start.2
  228.6 1.3 collective-permute-start.3
  229.9 3.9 fusion.45
  235.9 1.5 fusion.4
  237.4 263.4 %all-reduce.6.cloned.1.call-done = (f32[9,256,256]{2,1,0:T(8,128)}, f32[256,256]{0,1:T(8,128)}) async-done(((f32[9,256,256]{2,1,0:T(8,128)}, f32[256,256]{0,1:T(8,128)}), (f32[9,256,256]{2,1,0:T(8,128)}, f32[256,256]{0,1:T(8,128)})) %all-reduce.6.cloned.1.call-update) | async-done | bytes 2621456 | tf_op jit(solution)/shard_map/psum | solution.py:150
  500.8 1.7 dynamic-slice_multiply_fusion
  502.5 1.4 dynamic-slice_multiply_fusion.1
  (160 shorter events, 33.6 us)
Async XLA Ops:
  7.2 13.5 %copy-start = (bf16[9,256,256]{2,1,0:T(8,128)(2,1)S(1)}, bf16[9,256,256]{2,1,0:T(8,128)(2,1)}, u32[]{:S(2)}) copy-start(bf16[9,256,256]{2,1,0:T(8,128)(2,1)} %param.17) | copy-start | bytes 3538948
  7.2 13.2 %copy-start.1 = (bf16[2,4,64,256]{3,2,1,0:T(8,128)(2,1)S(1)}, bf16[2,4,64,256]{3,2,1,0:T(8,128)(2,1)}, u32[]{:S(2)}) copy-start(bf16[2,4,64,256]{3,2,1,0:T(8,128)(2,1)} %param.15) | copy-start | bytes 786436
  7.2 76.8 %all-gather.4.cloned.1.call-start = ((), (), s32[]{:S(2)}) async-start(), calls=%async_computation | async-start | bytes 8650752 | tf_op jit(solution)/shard_map/all_gather | solution.py:30
  8.2 6.8 %collective-permute-start = (bf16[2,1,64,256]{3,2,1,0:T(8,128)(2,1)S(1)}, bf16[2,1,64,256]{3,2,1,0:T(8,128)(2,1)S(1)}, u32[]{:S(2)}, u32[]{:S(2)}) collective-permute-start(bf16[2,1,64,256]{3,2,1,0:T(8,128)(2,1)S(1)} %get-tuple-element.436), channel_id=1, source_target_pairs={{0,1},{1,2},{2,3},{3,4},{4,5},{5,6},{6,7},{8,9},{9,10},{10,11},{11... | collective-permute-start | bytes 196616 | tf_op jit(solution)/shard_map/ppermute | solution.py:19
  12.1 6.2 %collective-permute-start.1 = (bf16[2,1,64,256]{3,2,1,0:T(8,128)(2,1)S(1)}, bf16[2,1,64,256]{3,2,1,0:T(8,128)(2,1)S(1)}, u32[]{:S(2)}, u32[]{:S(2)}) collective-permute-start(bf16[2,1,64,256]{3,2,1,0:T(8,128)(2,1)S(1)} %get-tuple-element.437), channel_id=1, source_target_pairs={{1,0},{2,1},{3,2},{4,3},{5,4},{6,5},{7,6},{9,8},{10,9},{11,10},{12... | collective-permute-start | bytes 196616 | tf_op jit(solution)/shard_map/ppermute | solution.py:21
  20.6 1.5 copy-start.2
  20.6 1.5 copy-start.4
  23.2 157.2 %all-gather.6.cloned.1.call-start = ((), (), s32[]{:S(2)}) async-start(), calls=%async_computation.1 | async-start | bytes 8650752 | tf_op jit(solution)/shard_map/all_gather | solution.py:30
  84.0 37.0 %copy-start.3 = (bf16[256,256]{1,0:T(8,128)(2,1)S(1)}, bf16[256,256]{1,0:T(8,128)(2,1)}, u32[]{:S(2)}) copy-start(bf16[256,256]{1,0:T(8,128)(2,1)} %param.18) | copy-start | bytes 393220
  84.0 37.0 %copy-start.5 = (bf16[2,4,64,256]{3,2,1,0:T(8,128)(2,1)S(1)}, bf16[2,4,64,256]{3,2,1,0:T(8,128)(2,1)}, u32[]{:S(2)}) copy-start(bf16[2,4,64,256]{3,2,1,0:T(8,128)(2,1)} %param.16) | copy-start | bytes 786436
  122.8 378.0 %all-reduce.6.cloned.1.call-start = ((), (), s32[]{:S(2)}) async-start(), calls=%async_computation.2 | async-start | bytes 5242880 | tf_op jit(solution)/shard_map/psum | solution.py:150
  225.1 8.7 %collective-permute-start.2 = (bf16[2,1,64,256]{3,2,1,0:T(8,128)(2,1)S(1)}, bf16[2,1,64,256]{3,2,1,0:T(8,128)(2,1)S(1)}, u32[]{:S(2)}, u32[]{:S(2)}) collective-permute-start(bf16[2,1,64,256]{3,2,1,0:T(8,128)(2,1)S(1)} %get-tuple-element.434), channel_id=1, source_target_pairs={{0,1},{1,2},{2,3},{3,4},{4,5},{5,6},{6,7},{8,9},{9,10},{10,11},{11... | collective-permute-start | bytes 196616 | tf_op jit(solution)/shard_map/ppermute | solution.py:19
  228.6 6.2 %collective-permute-start.3 = (bf16[2,1,64,256]{3,2,1,0:T(8,128)(2,1)S(1)}, bf16[2,1,64,256]{3,2,1,0:T(8,128)(2,1)S(1)}, u32[]{:S(2)}, u32[]{:S(2)}) collective-permute-start(bf16[2,1,64,256]{3,2,1,0:T(8,128)(2,1)S(1)} %get-tuple-element.435), channel_id=1, source_target_pairs={{1,0},{2,1},{3,2},{4,3},{5,4},{6,5},{7,6},{9,8},{10,9},{11,10},{12... | collective-permute-start | bytes 196616 | tf_op jit(solution)/shard_map/ppermute | solution.py:21
  234.9 1.0 copy-start.6
  234.9 0.9 copy-start.7
Sparse Core Ops, SparseCore 0:
  23.3 60.6 all-gather.3
  122.9 57.4 all-gather.5
  233.9 266.8 all-reduce.5
where the time goes:
time: 513 us; the launch traced here: 510 us
  waiting for transfers between devices  350 us (68%)
  other arithmetic  79.8 us (16%)
  blocking collectives  24.2 us (5%)
  local copies, waits for them, and re-layouts  22.5 us (4%)
  between operations  14.2 us (3%)
  starting transfers between devices  9.99 us (2%)
  matrix products  7.92 us (2%)
    psum x1, waiting for transfers between devices, local(): lax.psum((kernel_term, readout_term), ('tm', 'row'))  263 us
    all_gather x2, waiting for transfers between devices, carried_in(): pieces = jax.tree.map(lambda part: lax.all_gather(part, axis), value)  82.3 us
    select_n x62, other arithmetic, turn(): jnp.where(position < mine, new, old)  71.3 us
    all_gather x1, blocking collectives, carried_in(): pieces = jax.tree.map(lambda part: lax.all_gather(part, axis), value)  24.2 us
  transfers between devices with their start and end apart: 7, of which 5 were waited for; matrix products, arithmetic and copies ran while one was open for 4% of the time, Pallas kernels for 0%

commit v1 on v0

--- a/solution.py
+++ b/solution.py
@@ -147,7 +147,7 @@
     band_count = lax.axis_size("row")
     scaling = 1.0 / math.sqrt(cell_count * lax.axis_size("tm") * band_count)
     share_width = channels // band_count
-    kernel_all, readout_all = lax.psum((kernel_term, readout_term), ("tm", "row"))
+    kernel_all, readout_all = lax.psum(lax.psum((kernel_term, readout_term), "tm"), "row")
     offset_start = lax.axis_index("row") * share_width
     kernel_part = lax.dynamic_slice_in_dim(kernel_all, offset_start, share_width, 1)
     readout_part = lax.dynamic_slice_in_dim(readout_all, offset_start, share_width, 1)

time: 513 us -> 448 us (0.87)
  waiting for transfers between devices: 350 us -> 284 us
    psum x1 -> x2, waiting for transfers between devices: 263 us -> 194 us  [the longest x1 118 us: local(): lax.psum((kernel_term, readout_term), 'tm')]
  transfers between devices with their start and end apart: 7 -> 8, of which waited for: 5 -> 7; matrix products, arithmetic and copies ran while one was open for 4% -> 3% of each run, Pallas kernels for 0% -> 0%
where the time goes in v1:
time: 448 us; the launch traced here: 445 us
  waiting for transfers between devices  284 us (63%)
  other arithmetic  79.8 us (18%)
  blocking collectives  24.2 us (5%)
  local copies, waits for them, and re-layouts  22.6 us (5%)
  between operations  14.2 us (3%)
  starting transfers between devices  10 us (2%)
  matrix products  7.92 us (2%)
    psum x1, waiting for transfers between devices, local(): lax.psum((kernel_term, readout_term), 'tm')  118 us
    all_gather x2, waiting for transfers between devices, carried_in(): pieces = jax.tree.map(lambda part: lax.all_gather(part, axis), value)  82.3 us
    psum x1, waiting for transfers between devices, local(): lax.psum(lax.psum((kernel_term, readout_term), 'tm'), 'row')  76.2 us
    select_n x62, other arithmetic, turn(): jnp.where(position < mine, new, old)  71.3 us
    all_gather x1, blocking collectives, carried_in(): pieces = jax.tree.map(lambda part: lax.all_gather(part, axis), value)  24.2 us
  transfers between devices with their start and end apart: 8, of which 7 were waited for; matrix products, arithmetic and copies ran while one was open for 3% of the time, Pallas kernels for 0%

profile of v1, /device:TPU:2, one launch (start us, length us, event | category | flops | bytes accessed | tf_op | source)
XLA Modules:
  0.0 445.1 jit_solution(11240163577290987358)
XLA Ops:
  8.2 3.8 collective-permute-start
  12.1 1.3 collective-permute-start.1
  15.1 3.2 collective-permute-done.1
  23.3 24.2 %all-gather = f32[32,1,256]{2,1,0:T(1,128)S(1)} all-gather(f32[1,1,256]{2,1,0:T(1,128)S(1)} %slice_bitcast_fusion.12), channel_id=1, replica_groups=mesh['tm'=32,'row'=8] {'tm'}, dimensions={0}, use_global_device_ids=true | all-gather | bytes 33792 | tf_op jit(solution)/shard_map/all_gather | solution.py:30
  47.6 36.4 %all-gather.4.cloned.1.call-done = f32[32,4,64,256]{3,2,1,0:T(8,128)} async-done(((f32[1,4,64,256]{3,2,1,0:T(8,128)}), f32[32,4,64,256]{3,2,1,0:T(8,128)}) %all-gather.4.cloned.1.call-update) | async-done | bytes 8388624 | tf_op jit(solution)/shard_map/all_gather | solution.py:30
  84.0 36.9 %while.58 = (s32[]{:T(128)}, f32[4,64,256]{2,1,0:T(8,128)S(1)}, s32[]{:T(128)}, f32[32,256]{1,0:T(8,128)S(1)}, f32[32,4,64,256]{3,2,1,0:T(8,128)}, /*index=5*/s32[]{:T(128)}, s32[]{:T(128)}) while((s32[]{:T(128)}, f32[4,64,256]{2,1,0:T(8,128)S(1)}, s32[]{:T(128)}, f32[32,256]{1,0:T(8,128)S(1)}, f32[32,4,64,256]{3,2,1,0:T(8,128)}, ...), condition=%wide.region_4.5_spmd.clone, body=%wide.region_3.4_spmd.clone.sunk | while | flops 262148 | bytes 789609 | solution.py:42
  84.0 1.2 fusion.59
  85.2 1.1 fusion.59
  86.4 1.1 fusion.59
  87.6 1.1 fusion.59
  88.8 1.1 fusion.59
  90.0 1.1 fusion.59
  91.2 1.1 fusion.59
  92.4 1.1 fusion.59
  93.6 1.1 fusion.59
  94.7 1.1 fusion.59
  95.9 1.1 fusion.59
  97.1 1.1 fusion.59
  98.3 1.1 fusion.59
  99.5 1.1 fusion.59
  100.7 1.1 fusion.59
  101.9 1.1 fusion.59
  103.1 1.1 fusion.59
  104.3 1.1 fusion.59
  105.5 1.1 fusion.59
  106.6 1.1 fusion.59
  107.8 1.1 fusion.59
  109.0 1.1 fusion.59
  110.2 1.1 fusion.59
  111.4 1.1 fusion.59
  112.6 1.1 fusion.59
  113.8 1.1 fusion.59
  115.0 1.1 fusion.59
  116.2 1.1 fusion.59
  117.3 1.1 fusion.59
  118.5 1.1 fusion.59
  119.7 1.1 fusion.59
  123.2 3.3 copy.51
  126.5 2.8 copy.57
  129.3 4.3 copy.52
  134.6 45.9 %all-gather.6.cloned.1.call-done = f32[32,4,64,256]{3,2,1,0:T(8,128)} async-done(((f32[1,4,64,256]{3,2,1,0:T(8,128)}), f32[32,4,64,256]{3,2,1,0:T(8,128)}) %all-gather.6.cloned.1.call-update) | async-done | bytes 8388624 | tf_op jit(solution)/shard_map/all_gather | solution.py:30
  180.4 7.7 %rev.16 = f32[32,4,64,256]{3,2,1,0:T(8,128)} reverse(f32[32,4,64,256]{3,2,1,0:T(8,128)} %all-gather.6.cloned.1.call-done), dimensions={0} | reverse | bytes 16777216 | tf_op jit(solution)/shard_map/rev | solution.py:32
  188.2 36.8 %while.60 = (s32[]{:T(128)}, f32[4,64,256]{2,1,0:T(8,128)S(1)}, s32[]{:T(128)}, f32[32,256]{1,0:T(8,128)S(1)}, f32[32,4,64,256]{3,2,1,0:T(8,128)}, /*index=5*/s32[]{:T(128)}, s32[]{:T(128)}) while((s32[]{:T(128)}, f32[4,64,256]{2,1,0:T(8,128)S(1)}, s32[]{:T(128)}, f32[32,256]{1,0:T(8,128)S(1)}, f32[32,4,64,256]{3,2,1,0:T(8,128)}, ...), condition=%wide.region_9.10_spmd.clone, body=%wide.region_8.9_spmd.clone.sunk | while | flops 262148 | bytes 789609 | solution.py:42
  189.4 1.1 fusion.60
  190.5 1.1 fusion.60
  191.7 1.1 fusion.60
  192.9 1.1 fusion.60
  194.1 1.1 fusion.60
  195.3 1.1 fusion.60
  196.5 1.1 fusion.60
  197.7 1.1 fusion.60
  198.9 1.1 fusion.60
  200.1 1.1 fusion.60
  201.2 1.1 fusion.60
  202.4 1.1 fusion.60
  225.1 3.9 fusion.45
  229.0 117.8 %all-reduce.8.cloned.1.call-done = (f32[9,256,256]{2,1,0:T(8,128)}, f32[256,256]{0,1:T(8,128)}) async-done(((f32[9,256,256]{2,1,0:T(8,128)}, f32[256,256]{0,1:T(8,128)}), (f32[9,256,256]{2,1,0:T(8,128)}, f32[256,256]{0,1:T(8,128)})) %all-reduce.8.cloned.1.call-update) | async-done | bytes 2621456 | tf_op jit(solution)/shard_map/psum | solution.py:150
  346.9 3.5 collective-permute-start.2
  350.4 1.3 collective-permute-start.3
  352.3 4.3 collective-permute-done.3
  357.7 1.5 fusion.4
  359.2 76.2 %all-reduce.10.cloned.1.call-done = (f32[9,256,256]{2,1,0:T(8,128)}, f32[256,256]{0,1:T(8,128)}) async-done(((f32[9,256,256]{2,1,0:T(8,128)}, f32[256,256]{0,1:T(8,128)}), (f32[9,256,256]{2,1,0:T(8,128)}, f32[256,256]{0,1:T(8,128)})) %all-reduce.10.cloned.1.call-update) | async-done | bytes 2621456 | tf_op jit(solution)/shard_map/psum | solution.py:150
  435.5 1.7 dynamic-slice_multiply_fusion
  437.2 1.4 dynamic-slice_multiply_fusion.1
  (163 shorter events, 35.6 us)
Async XLA Ops:
  7.2 13.5 %copy-start = (bf16[9,256,256]{2,1,0:T(8,128)(2,1)S(1)}, bf16[9,256,256]{2,1,0:T(8,128)(2,1)}, u32[]{:S(2)}) copy-start(bf16[9,256,256]{2,1,0:T(8,128)(2,1)} %param.17) | copy-start | bytes 3538948
  7.2 13.2 %copy-start.1 = (bf16[2,4,64,256]{3,2,1,0:T(8,128)(2,1)S(1)}, bf16[2,4,64,256]{3,2,1,0:T(8,128)(2,1)}, u32[]{:S(2)}) copy-start(bf16[2,4,64,256]{3,2,1,0:T(8,128)(2,1)} %param.15) | copy-start | bytes 786436
  7.2 76.8 %all-gather.4.cloned.1.call-start = ((), (), s32[]{:S(2)}) async-start(), calls=%async_computation | async-start | bytes 8650752 | tf_op jit(solution)/shard_map/all_gather | solution.py:30
  8.2 6.8 %collective-permute-start = (bf16[2,1,64,256]{3,2,1,0:T(8,128)(2,1)S(1)}, bf16[2,1,64,256]{3,2,1,0:T(8,128)(2,1)S(1)}, u32[]{:S(2)}, u32[]{:S(2)}) collective-permute-start(bf16[2,1,64,256]{3,2,1,0:T(8,128)(2,1)S(1)} %get-tuple-element.438), channel_id=1, source_target_pairs={{0,1},{1,2},{2,3},{3,4},{4,5},{5,6},{6,7},{8,9},{9,10},{10,11},{11... | collective-permute-start | bytes 196616 | tf_op jit(solution)/shard_map/ppermute | solution.py:19
  12.1 6.2 %collective-permute-start.1 = (bf16[2,1,64,256]{3,2,1,0:T(8,128)(2,1)S(1)}, bf16[2,1,64,256]{3,2,1,0:T(8,128)(2,1)S(1)}, u32[]{:S(2)}, u32[]{:S(2)}) collective-permute-start(bf16[2,1,64,256]{3,2,1,0:T(8,128)(2,1)S(1)} %get-tuple-element.439), channel_id=1, source_target_pairs={{1,0},{2,1},{3,2},{4,3},{5,4},{6,5},{7,6},{9,8},{10,9},{11,10},{12... | collective-permute-start | bytes 196616 | tf_op jit(solution)/shard_map/ppermute | solution.py:21
  20.6 1.5 copy-start.2
  20.6 1.5 copy-start.4
  23.2 157.2 %all-gather.6.cloned.1.call-start = ((), (), s32[]{:S(2)}) async-start(), calls=%async_computation.1 | async-start | bytes 8650752 | tf_op jit(solution)/shard_map/all_gather | solution.py:30
  84.0 37.0 %copy-start.3 = (bf16[256,256]{1,0:T(8,128)(2,1)S(1)}, bf16[256,256]{1,0:T(8,128)(2,1)}, u32[]{:S(2)}) copy-start(bf16[256,256]{1,0:T(8,128)(2,1)} %param.18) | copy-start | bytes 393220
  84.0 37.0 %copy-start.5 = (bf16[2,4,64,256]{3,2,1,0:T(8,128)(2,1)S(1)}, bf16[2,4,64,256]{3,2,1,0:T(8,128)(2,1)}, u32[]{:S(2)}) copy-start(bf16[2,4,64,256]{3,2,1,0:T(8,128)(2,1)} %param.16) | copy-start | bytes 786436
  122.8 224.0 %all-reduce.8.cloned.1.call-start = ((), (), s32[]{:S(2)}) async-start(), calls=%async_computation.2 | async-start | bytes 5242880 | tf_op jit(solution)/shard_map/psum | solution.py:150
  229.0 206.5 %all-reduce.10.cloned.1.call-start = ((), (), s32[]{:S(2)}) async-start(), calls=%async_computation.3 | async-start | bytes 5242880 | tf_op jit(solution)/shard_map/psum | solution.py:150
  346.9 5.4 %collective-permute-start.2 = (bf16[2,1,64,256]{3,2,1,0:T(8,128)(2,1)S(1)}, bf16[2,1,64,256]{3,2,1,0:T(8,128)(2,1)S(1)}, u32[]{:S(2)}, u32[]{:S(2)}) collective-permute-start(bf16[2,1,64,256]{3,2,1,0:T(8,128)(2,1)S(1)} %get-tuple-element.436), channel_id=1, source_target_pairs={{0,1},{1,2},{2,3},{3,4},{4,5},{5,6},{6,7},{8,9},{9,10},{10,11},{11... | collective-permute-start | bytes 196616 | tf_op jit(solution)/shard_map/ppermute | solution.py:19
  350.4 6.2 %collective-permute-start.3 = (bf16[2,1,64,256]{3,2,1,0:T(8,128)(2,1)S(1)}, bf16[2,1,64,256]{3,2,1,0:T(8,128)(2,1)S(1)}, u32[]{:S(2)}, u32[]{:S(2)}) collective-permute-start(bf16[2,1,64,256]{3,2,1,0:T(8,128)(2,1)S(1)} %get-tuple-element.437), channel_id=1, source_target_pairs={{1,0},{2,1},{3,2},{4,3},{5,4},{6,5},{7,6},{9,8},{10,9},{11,10},{12... | collective-permute-start | bytes 196616 | tf_op jit(solution)/shard_map/ppermute | solution.py:21
  356.7 1.0 copy-start.6
  356.7 0.9 copy-start.7
Sparse Core Ops, SparseCore 0:
  23.3 60.6 all-gather.3
  123.0 57.4 all-gather.5
  229.1 117.7 all-reduce.7
  349.2 86.2 all-reduce.9
